TPU v7x, 32 devices: a whole 2x2x4 slice. The times are simulated.
32 devices in a mesh: row: 4 (over y, core), col: 8 (over z, x).
Axes of the slice: x: 2, y: 2, z: 4, core: 2. Of those that a mesh axis runs over, the one named last changes fastest.
Arguments:
- gram_matrix: float32 [12288, 12288], P('row', 'col'), may hold values from -1 to 16, as said below
- targets: float32 [10, 12288], P(None, ('row', 'col')), may hold values from -10 to 10
Outputs:
- solution: float32 [10, 12288], P(None, ('row', 'col'))
- residual: float32 [10, 12288], P(None, ('row', 'col'))
Inputs may be any that keep to these rules, and one draw needn't show every extreme that they name: With its columns put back in sample order as in the first step, gram_matrix is symmetric positive definite.
All inputs are finite; a program needn't handle non-finite values.
Results may differ from a plain program's by a relative error of at most 0.0003.
Values sent between devices are 32-bit elements; how exact they have to be, the bound alone decides.
A program may use at most 64 MiB of HBM per device.

v0:
```python
import jax
import jax.numpy as jnp
from jax import lax
from jax.sharding import PartitionSpec as P

ITERS = 2


def apply_gram(gram_matrix, vectors):
    partial_value = jnp.dot(
        vectors, gram_matrix, precision=lax.Precision.HIGHEST, preferred_element_type=jnp.float32
    )
    mapped = lax.psum_scatter(partial_value, "row", scatter_dimension=1, tiled=True)
    mapped = lax.all_gather(mapped, "col", axis=1, tiled=True)
    return mapped


def class_sums(values):
    return lax.psum(values, "row")


def shards(gram_matrix, targets):
    piece_len = targets.shape[1]
    known = lax.all_gather(targets, "col", axis=1, tiled=True)
    solution = jnp.zeros_like(known)
    residual = known
    direction = known
    norm_now = class_sums(jnp.sum(residual * residual, axis=1))
    for iteration in range(ITERS):
        mapped = apply_gram(gram_matrix, direction)
        step_size = norm_now / class_sums(jnp.sum(direction * mapped, axis=1))
        solution = solution + step_size[:, None] * direction
        residual = residual - step_size[:, None] * mapped
        norm_next = class_sums(jnp.sum(residual * residual, axis=1))
        direction = residual + (norm_next / norm_now)[:, None] * direction
        norm_now = norm_next
    offset = lax.axis_index("col") * piece_len
    solution = lax.dynamic_slice_in_dim(solution, offset, piece_len, 1)
    residual = lax.dynamic_slice_in_dim(residual, offset, piece_len, 1)
    return (solution, residual)


def solution(mesh):
    in_specs = (P("row", "col"), P(None, ("row", "col")))
    out_specs = (P(None, ("row", "col")), P(None, ("row", "col")))
    return jax.shard_map(shards, mesh=mesh, in_specs=in_specs, out_specs=out_specs, check_vma=False)
```

profile of v0, /device:TPU:0, one launch (start us, length us, event | category | flops | bytes accessed | tf_op | source)
XLA Modules:
  0.0 193.7 jit_solution(8119526722495758098)
XLA Ops:
  7.2 0.0 reduce-scatter.3.cloned.1.call-start
  7.2 32.7 %all_gather.9 = f32[10,3072]{1,0:T(8,128)S(1)} all-gather(f32[10,384]{1,0:T(8,128)} %param.3), channel_id=1, replica_groups=mesh['row'=4,'col'=8] {'col'}, dimensions={1}, use_global_device_ids=true | all-gather | bytes 138240 | tf_op jit(solution)/shard_map/all_gather | solution.py:24
  39.9 12.6 %fusion.1 = f32[10,1536]{1,0:T(8,128)} fusion(f32[10,3072]{1,0:T(8,128)S(1)} %all_gather.9, f32[3072,1536]{1,0:T(8,128)} %param.2), kind=kOutput, calls=%fused_computation.11 | convolution fusion | flops 566231040 | bytes 19058688 | tf_op jit(solution)/shard_map/dot_general | solution.py:10
  52.5 0.0 reduce-scatter.3.cloned.1.call-update
  52.5 0.0 reduce-scatter.5.cloned.1.call-start
  52.5 20.6 %reduce-scatter.3.cloned.1.call-done = f32[10,384]{1,0:T(8,128)} async-done(((f32[10,1536]{1,0:T(8,128)}), f32[10,384]{1,0:T(8,128)}) %reduce-scatter.3.cloned.1.call-update) | async-done | bytes 15376 | tf_op jit(solution)/shard_map/reduce_scatter | solution.py:13
  73.2 30.9 %all_gather.10 = f32[10,3072]{1,0:T(8,128)S(1)} all-gather(f32[10,384]{1,0:T(8,128)} %reduce-scatter.3.cloned.1.call-done), channel_id=1, replica_groups=mesh['row'=4,'col'=8] {'col'}, dimensions={1}, use_global_device_ids=true | all-gather | bytes 138240 | tf_op jit(solution)/shard_map/all_gather | solution.py:14
  104.1 0.2 multiply_reduce_fusion.2
  104.3 5.9 %all-reduce = (f32[10]{0:T(128)S(1)}, f32[10]{0:T(128)S(1)}) all-reduce(f32[10]{0:T(128)S(1)} %get-tuple-element.3, f32[10]{0:T(128)S(1)} %get-tuple-element.2), channel_id=1, replica_groups=mesh['row'=4,'col'=8] {'row'}, use_global_device_ids=true, to_apply=%region_1.0 | all-reduce | flops 20 | bytes 160 | tf_op jit(solution)/shard_map/psum | solution.py:19
  110.2 0.2 multiply_reduce_fusion.1
  110.4 5.8 %psum.30 = f32[10]{0:T(128)S(1)} all-reduce(f32[10]{0:T(128)S(1)} %get-tuple-element.6), channel_id=1, replica_groups=mesh['row'=4,'col'=8] {'row'}, use_global_device_ids=true, to_apply=%region_6.0 | all-reduce | flops 10 | bytes 80 | tf_op jit(solution)/shard_map/psum | solution.py:19
  116.2 0.1 multiply_add_fusion
  116.3 12.6 %fusion.2 = f32[10,1536]{1,0:T(8,128)} fusion(f32[10,3072]{1,0:T(8,128)S(1)} %multiply_add_fusion, f32[3072,1536]{1,0:T(8,128)} %param.2), kind=kOutput, calls=%fused_computation.12 | convolution fusion | flops 566231040 | bytes 19058688 | tf_op jit(solution)/shard_map/dot_general | solution.py:10
  128.9 0.0 reduce-scatter.5.cloned.1.call-update
  128.9 20.3 %reduce-scatter.5.cloned.1.call-done = f32[10,384]{1,0:T(8,128)} async-done(((f32[10,1536]{1,0:T(8,128)}), f32[10,384]{1,0:T(8,128)}) %reduce-scatter.5.cloned.1.call-update) | async-done | bytes 15376 | tf_op jit(solution)/shard_map/reduce_scatter | solution.py:13
  149.2 30.9 %all_gather.11 = f32[10,3072]{1,0:T(8,128)S(1)} all-gather(f32[10,384]{1,0:T(8,128)} %reduce-scatter.5.cloned.1.call-done), channel_id=1, replica_groups=mesh['row'=4,'col'=8] {'col'}, dimensions={1}, use_global_device_ids=true | all-gather | bytes 138240 | tf_op jit(solution)/shard_map/all_gather | solution.py:14
  180.1 0.1 multiply_reduce_fusion
  180.2 5.9 %psum.31 = f32[10]{0:T(128)S(1)} all-reduce(f32[10]{0:T(128)S(1)} %multiply_reduce_fusion), channel_id=1, replica_groups=mesh['row'=4,'col'=8] {'row'}, use_global_device_ids=true, to_apply=%region_9.0 | all-reduce | flops 10 | bytes 80 | tf_op jit(solution)/shard_map/psum | solution.py:19
  186.2 0.7 dynamic-slice_subtract_fusion
  (3 shorter events, 0.0 us)
Async XLA Ops:
  7.2 66.0 %reduce-scatter.3.cloned.1.call-start = ((), (), s32[]{:S(2)}) async-start(), calls=%async_computation.2 | async-start | bytes 122880 | tf_op jit(solution)/shard_map/reduce_scatter | solution.py:13
  52.5 96.7 %reduce-scatter.5.cloned.1.call-start = ((), (), s32[]{:S(2)}) async-start(), calls=%async_computation.3 | async-start | bytes 122880 | tf_op jit(solution)/shard_map/reduce_scatter | solution.py:13
Sparse Core Ops, SparseCore 0:
  52.6 20.5 reduce-scatter.2
  129.0 20.1 reduce-scatter.4
where the time goes:
time: 194 us
  blocking collectives  112 us (58%)
  waiting for transfers between devices  41 us (21%)
  matrix products  25.2 us (13%)
  between operations  14.1 us (7%)
    all_gather x2, blocking collectives, apply_gram(): mapped = lax.all_gather(mapped, 'col', axis=1, tiled=True)  61.8 us
    reduce_scatter x2, waiting for transfers between devices, apply_gram(): lax.psum_scatter(partial_value, 'row', scatter_dimension=1, tiled=True)  40.9 us
    all_gather x1, blocking collectives, shards(): known = lax.all_gather(targets, 'col', axis=1, tiled=True)  32.7 us
    dot_general x2, matrix products, apply_gram(): jnp.dot(vectors, gram_matrix, precision=lax.Precision.HIGHEST, preferred_...  25.2 us
    psum x3, blocking collectives, class_sums(): return lax.psum(values, 'row')  17.6 us
  transfers between devices with their start and end apart: 2, of which 2 were waited for; matrix products, arithmetic and copies ran while one was open for 0% of the time, Pallas kernels for 0%

commit v1 on v0

--- a/solution.py
+++ b/solution.py
@@ -1,9 +1,333 @@
+import functools
+
 import jax
 import jax.numpy as jnp
 from jax import lax
+from jax.experimental import pallas as pl
+from jax.experimental.pallas import tpu as pltpu
 from jax.sharding import PartitionSpec as P
 
 ITERS = 2
+LANES = 128
+SUB = 8
+DEPTH = 256
+MESH = pl.DeviceIdType.MESH
+F32 = jnp.float32
+BF16 = jnp.bfloat16
+
+
+def dot(a, b):
+    return lax.dot_general(a, b, (((1,), (0,)), ((), ())), preferred_element_type=F32)
+
+
+def halves(x):
+    high = x.astype(BF16)
+    return high, (x - high.astype(F32)).astype(BF16)
+
+
+def kernel(
+    n_row, n_col, classes, piece, group,
+    gram, targets, sol_out, res_out,
+    stage, high, low, acc, vec, wide,
+    t_col, t_row, w_part, w_col, w_row, m_part, moments, finals,
+    gram_sem, s_tcol, r_tcol, s_trow, r_trow, s_rs, r_rs, s_wcol, r_wcol, s_wrow, r_wrow,
+    s_rs2, r_rs2, s_mom, r_mom, s_fin, r_fin,
+):
+    row, col = lax.axis_index("row"), lax.axis_index("col")
+    rest = classes - SUB
+    tiles = piece // LANES
+    n_dev = n_row * n_col
+    n_group = n_col // group
+    own_group = col // group
+    depth = group * piece
+    order = [0]
+    for k in range(1, n_group):
+        order.append((k + 1) // 2 if k % 2 else n_group - k // 2)
+    groups = [lax.rem(own_group + k, n_group) for k in order]
+
+    for i in range(n_group):
+        pltpu.make_async_copy(
+            gram.at[pl.ds(pl.multiple_of(groups[i] * depth, DEPTH), depth)], stage.at[i], gram_sem.at[i]
+        ).start()
+
+    barrier = pltpu.get_barrier_semaphore()
+
+    def greet(k, carry):
+        other = lax.rem(row * n_col + col + k, n_dev)
+        pl.semaphore_signal(barrier, inc=1, device_id=(other // n_col, lax.rem(other, n_col)), device_id_type=MESH)
+        return carry
+
+    lax.fori_loop(1, n_dev, greet, 0)
+
+    rows8 = lax.broadcasted_iota(jnp.int32, (SUB, LANES), 0)
+
+    def pack(x):
+        extra = jnp.zeros((SUB, LANES), F32)
+        for i in range(tiles):
+            part = x[SUB:, i * LANES:(i + 1) * LANES]
+            if i:
+                part = pltpu.roll(part, rest * i, 0)
+            extra = jnp.where((rows8 >= rest * i) & (rows8 < rest * (i + 1)), part, extra)
+        return jnp.concatenate([x[:SUB], extra], axis=1)
+
+    def unpack(y):
+        extra = y[:, piece:]
+        parts = []
+        for i in range(tiles):
+            part = pltpu.roll(extra, SUB - rest * i, 0) if i else extra
+            parts.append(jnp.where(rows8 < rest, part, 0.0))
+        return jnp.concatenate([y[:, :piece], jnp.concatenate(parts, axis=1)], axis=0)
+
+    def to_col(src, dst, send, recv, k):
+        return pltpu.make_async_remote_copy(
+            src_ref=src, dst_ref=dst, send_sem=send.at[k], recv_sem=recv.at[k],
+            device_id=(row, lax.rem(col + k, n_col)), device_id_type=MESH)
+
+    def to_row(src, dst, send, recv, k):
+        return pltpu.make_async_remote_copy(
+            src_ref=src, dst_ref=dst, send_sem=send.at[k], recv_sem=recv.at[k],
+            device_id=(lax.rem(row + k, n_row), col), device_id_type=MESH)
+
+    started = []
+
+    def go(copy):
+        copy.start()
+        started.append(copy)
+        return copy
+
+    wide[...] = jnp.zeros_like(wide)
+    wide[0:classes, :] = targets[...]
+    mine_t = wide[...]
+    t_col[0] = pack(mine_t)
+    acc[...] = jnp.zeros_like(acc)
+    pl.semaphore_wait(barrier, n_dev - 1)
+
+    col_t = {k: go(to_col(t_col.at[0], t_col.at[k], s_tcol, r_tcol, k)) for k in range(1, n_col)}
+    row_t = {k: go(to_row(t_col.at[0], t_row.at[k], s_trow, r_trow, k)) for k in range(1, n_row)}
+
+    def gather(i, pieces, send, recv):
+        for j in range(group):
+            source = groups[i] * group + j
+            slot = lax.rem(col - source + n_col, n_col)
+
+            @pl.when(slot != 0)
+            def _():
+                to_col(pieces.at[0], pieces.at[slot], send, recv, slot).wait_recv()
+
+            x = unpack(pieces[slot])
+            a, b = halves(x)
+            vec[i, :, j * piece:(j + 1) * piece] = jnp.concatenate([a, b], axis=0)
+
+    def accumulate(v, h, l):
+        both = dot(v, h)
+        acc[...] += both[:16] + both[16:] + dot(v[:16], l)
+
+    for i in range(n_group):
+        pltpu.make_async_copy(gram.at[pl.ds(0, depth)], stage.at[i], gram_sem.at[i]).wait()
+        gather(i, t_col, s_tcol, r_tcol)
+
+        def first(j, carry, i=i):
+            off = pl.ds(pl.multiple_of(j * DEPTH, DEPTH), DEPTH)
+            h, l = halves(stage[i, off, :])
+            high[i, off, :] = h
+            low[i, off, :] = l
+            accumulate(vec[i, :, off], h, l)
+            return carry
+
+        lax.fori_loop(0, depth // DEPTH, first, 0)
+
+    def columns(k):
+        r = lax.rem(row - k + n_row, n_row)
+        return pl.ds(pl.multiple_of(r * piece, LANES), piece)
+
+    def scatter(parts, send, recv):
+        copies = {}
+        for k in range(1, n_row):
+            r = lax.rem(row + k, n_row)
+            parts[n_row + k] = pack(acc[:, pl.ds(pl.multiple_of(r * piece, LANES), piece)])
+            copies[k] = go(to_row(parts.at[n_row + k], parts.at[k], send, recv, k))
+        return copies
+
+    rs = scatter(w_part, s_rs, r_rs)
+    total = pack(acc[:, columns(0)])
+    for k in range(1, n_row):
+        rs[k].wait_recv()
+        total = total + w_part[k]
+    w_col[0] = total
+    col_w = {k: go(to_col(w_col.at[0], w_col.at[k], s_wcol, r_wcol, k)) for k in range(1, n_col)}
+    row_w = {k: go(to_row(w_col.at[0], w_row.at[k], s_wrow, r_wrow, k)) for k in range(1, n_row)}
+    acc[...] = jnp.zeros_like(acc)
+    mine_w = unpack(total)
+
+    ts, ws = [mine_t], [mine_w]
+    for k in range(1, n_row):
+        row_t[k].wait_recv()
+        row_w[k].wait_recv()
+        ts.append(unpack(t_row[k]))
+        ws.append(unpack(w_row[k]))
+
+    def inner(xs, ys):
+        value = xs[0] * ys[0]
+        for x, y in zip(xs[1:], ys[1:]):
+            value = value + x * y
+        return jnp.sum(value, axis=1, keepdims=True)
+
+    lane = lax.broadcasted_iota(jnp.int32, (16, LANES), 1)
+    sub = lax.broadcasted_iota(jnp.int32, (16, LANES), 0)
+
+    def to_lanes(values):
+        out = jnp.zeros((16, LANES), F32)
+        for m, value in enumerate(values):
+            out = jnp.where(lane == sub + 16 * m, value, out)
+        return jnp.sum(out, axis=0, keepdims=True)
+
+    def from_lanes(line, m):
+        full = jnp.broadcast_to(line, (16, LANES))
+        return jnp.sum(jnp.where(lane == sub + 16 * m, full, 0.0), axis=1, keepdims=True)
+
+    tt, tw, ww = inner(ts, ts), inner(ts, ws), inner(ws, ws)
+    guess = jnp.where(ww > 0.0, tw / jnp.where(ww > 0.0, ww, 1.0), 0.0)
+    rs0 = [t - guess * w for t, w in zip(ts, ws)]
+    rr, rw = inner(rs0, rs0), inner(rs0, ws)
+    moments[0] = to_lanes([tt, tw, ww, guess, rr, rw])
+    col_m = {k: go(to_col(moments.at[0], moments.at[k], s_mom, r_mom, k)) for k in range(1, n_col)}
+
+    for i in range(n_group):
+        gather(i, w_col, s_wcol, r_wcol)
+
+        def second(j, carry, i=i):
+            off = pl.ds(pl.multiple_of(j * DEPTH, DEPTH), DEPTH)
+            accumulate(vec[i, :, off], high[i, off, :], low[i, off, :])
+            return carry
+
+        lax.fori_loop(0, depth // DEPTH, second, 0)
+
+    rs2 = scatter(m_part, s_rs2, r_rs2)
+
+    for k in range(1, n_col):
+        col_m[k].wait_recv()
+    known = [[from_lanes(moments[k], m) for m in range(6)] for k in range(n_col)]
+
+    def add(values):
+        out = values[0]
+        for v in values[1:]:
+            out = out + v
+        return out
+
+    norm0 = add([m[0] for m in known])
+    t_k_t = add([m[1] for m in known])
+    step0 = norm0 / t_k_t
+    shift = [step0 - m[3] for m in known]
+    norm1 = add([m[4] - d * (2.0 * m[5] - d * m[2]) for m, d in zip(known, shift)])
+    r_w = add([m[5] - d * m[2] for m, d in zip(known, shift)])
+    beta = norm1 / norm0
+
+    def direction(t, w):
+        r = t - step0 * w
+        return r, r + beta * t
+
+    ds = [direction(t, w)[1] for t, w in zip(ts, ws)]
+    ps = [acc[:, columns(k)] for k in range(n_row)]
+    finals[0] = to_lanes([inner(ds, ps)])
+
+    def fin(k):
+        other = lax.rem(row * n_col + col + k, n_dev)
+        return pltpu.make_async_remote_copy(
+            src_ref=finals.at[0], dst_ref=finals.at[k], send_sem=s_fin.at[k], recv_sem=r_fin.at[k],
+            device_id=(other // n_col, lax.rem(other, n_col)), device_id_type=MESH)
+
+    def fin_start(k, carry):
+        fin(k).start()
+        return carry
+
+    lax.fori_loop(1, n_dev, fin_start, 0)
+
+    total2 = pack(acc[:, columns(0)])
+    for k in range(1, n_row):
+        rs2[k].wait_recv()
+        total2 = total2 + m_part[k]
+    w2 = unpack(total2)
+    r1, d1 = direction(mine_t, mine_w)
+    mapped = (1.0 + beta) * mine_w - step0 * w2
+
+    def fin_wait(k, carry):
+        fin(k).wait_recv()
+        return carry
+
+    lax.fori_loop(1, n_dev, fin_wait, 0)
+    d_w2 = from_lanes(jnp.sum(finals[...], axis=0), 0)
+    step1 = norm1 / ((1.0 + beta) * (r_w + beta * t_k_t) - step0 * d_w2)
+    wide[...] = step0 * mine_t + step1 * d1
+    sol_out[...] = wide[0:classes, :]
+    wide[...] = r1 - step1 * mapped
+    res_out[...] = wide[0:classes, :]
+
+    for copy in started:
+        copy.wait_send()
+
+    def fin_sent(k, carry):
+        fin(k).wait_send()
+        return carry
+
+    lax.fori_loop(1, n_dev, fin_sent, 0)
+
+
+def fused(n_row, n_col, gram_matrix, targets):
+    classes, piece = targets.shape
+    height, width = gram_matrix.shape
+    group = 1 if piece % DEPTH == 0 else 2
+    n_group = n_col // group
+    depth = group * piece
+    packed = (SUB, piece + LANES)
+    dma = pltpu.SemaphoreType.DMA
+    n_dev = n_row * n_col
+    vmem = pl.BlockSpec(memory_space=pltpu.VMEM)
+    return pl.pallas_call(
+        functools.partial(kernel, n_row, n_col, classes, piece, group),
+        out_shape=[jax.ShapeDtypeStruct(targets.shape, F32)] * 2,
+        in_specs=[pl.BlockSpec(memory_space=pl.ANY), vmem],
+        out_specs=[vmem, vmem],
+        scratch_shapes=[
+            pltpu.VMEM((n_group, depth, width), F32),
+            pltpu.VMEM((n_group, depth, width), BF16),
+            pltpu.VMEM((n_group, depth, width), BF16),
+            pltpu.VMEM((16, width), F32),
+            pltpu.VMEM((n_group, 32, depth), BF16),
+            pltpu.VMEM((16, piece), F32),
+            pltpu.VMEM((n_col,) + packed, F32),
+            pltpu.VMEM((n_row,) + packed, F32),
+            pltpu.VMEM((2 * n_row,) + packed, F32),
+            pltpu.VMEM((n_col,) + packed, F32),
+            pltpu.VMEM((n_row,) + packed, F32),
+            pltpu.VMEM((2 * n_row,) + packed, F32),
+            pltpu.VMEM((n_col, 1, LANES), F32),
+            pltpu.VMEM((n_dev, 1, LANES), F32),
+            dma((n_group,)),
+            dma((n_col,)), dma((n_col,)), dma((n_row,)), dma((n_row,)),
+            dma((n_row,)), dma((n_row,)),
+            dma((n_col,)), dma((n_col,)), dma((n_row,)), dma((n_row,)),
+            dma((n_row,)), dma((n_row,)),
+            dma((n_col,)), dma((n_col,)),
+            dma((n_dev,)), dma((n_dev,)),
+        ],
+        compiler_params=pltpu.CompilerParams(
+            collective_id=0, has_side_effects=True, vmem_limit_bytes=60 * 2**20
+        ),
+    )(gram_matrix, targets)
+
+
+def fits(n_row, n_col, gram_matrix, targets):
+    classes, piece = targets.shape
+    rest = classes - SUB
+    group = 1 if piece % DEPTH == 0 else 2
+    return (
+        piece % LANES == 0
+        and 0 < rest <= SUB
+        and rest * (piece // LANES) <= SUB
+        and n_col % group == 0
+        and (group * piece) % DEPTH == 0
+        and gram_matrix.size * 8 <= 48 * 2**20
+    )
 
 
 def apply_gram(gram_matrix, vectors):
@@ -41,6 +365,13 @@
 
 
 def solution(mesh):
+    n_row, n_col = mesh.shape["row"], mesh.shape["col"]
+
+    def local(gram_matrix, targets):
+        if fits(n_row, n_col, gram_matrix, targets):
+            return tuple(fused(n_row, n_col, gram_matrix, targets))
+        return shards(gram_matrix, targets)
+
     in_specs = (P("row", "col"), P(None, ("row", "col")))
     out_specs = (P(None, ("row", "col")), P(None, ("row", "col")))
-    return jax.shard_map(shards, mesh=mesh, in_specs=in_specs, out_specs=out_specs, check_vma=False)
+    return jax.shard_map(local, mesh=mesh, in_specs=in_specs, out_specs=out_specs, check_vma=False)

time: 194 us -> 37.4 us (0.19)
  blocking collectives: 112 us -> 0 us
  waiting for transfers between devices: 41 us -> 0 us
  Pallas kernels: 0 us -> 33.8 us
  matrix products: 25.2 us -> 0 us
  between operations: 14.1 us -> 0.64 us
  local copies, waits for them, and re-layouts: 0 us -> 2.69 us
    all_gather x3 -> x0, blocking collectives: 94.5 us -> none  [the longest x2 61.8 us: apply_gram(): mapped = lax.all_gather(mapped, 'col', axis=1, tiled=True)]
    reduce_scatter x2 -> x0, waiting for transfers between devices: 40.9 us -> none  [apply_gram(): lax.psum_scatter(partial_value, 'row', scatter_dimension=1, tiled=True)]
    pallas_call x0 -> x1, Pallas kernels: none -> 33.8 us  [fused(): pl.pallas_call(functools.partial(kernel, n_row, n_col, classes, piece, gr...]
    dot_general x2 -> x0, matrix products: 25.2 us -> none  [apply_gram(): jnp.dot(vectors, gram_matrix, precision=lax.Precision.HIGHEST, preferred_...]
    psum x3 -> x0, blocking collectives: 17.6 us -> none  [class_sums(): return lax.psum(values, 'row')]
    unnamed x0 -> x2, local copies, waits for them, and re-layouts: none -> 2.69 us
  transfers between devices with their start and end apart: 2 -> 0, of which waited for: 2 -> 0; matrix products, arithmetic and copies ran while one was open for 0% -> 0% of each run, Pallas kernels for 0% -> 0%
where the time goes in v1:
time: 37.4 us; the launch traced here: 37.1 us
  Pallas kernels  33.8 us (90%)
  local copies, waits for them, and re-layouts  2.69 us (7%)
  between operations  0.64 us (2%)
    pallas_call x1, Pallas kernels, fused(): pl.pallas_call(functools.partial(kernel, n_row, n_col, classes, piece, gr...  33.8 us
    unnamed x2, local copies, waits for them, and re-layouts  2.69 us

profile of v1, /device:TPU:0, one launch (start us, length us, event | category | flops | bytes accessed | tf_op | source)
XLA Modules:
  0.0 37.1 jit_solution(15933705397065206561)
XLA Ops:
  0.6 33.8 %shard_map.41 = (f32[10,384]{1,0:T(8,128)}, f32[10,384]{1,0:T(8,128)}) custom-call(f32[3072,1536]{1,0:T(8,128)} %gram.1, f32[10,384]{1,0:T(8,128)} %targets.1), custom_call_target="tpu_custom_call" | custom-call | tf_op jit(solution)/shard_map/pallas_call | solution.py:285
  34.4 1.3 %copy.6 = f32[10,384]{1,0:T(8,128)} copy(f32[10,384]{1,0:T(8,128)} %get-tuple-element.4) | data formatting | bytes 30720
  35.7 1.3 %copy.7 = f32[10,384]{1,0:T(8,128)} copy(f32[10,384]{1,0:T(8,128)} %get-tuple-element.5) | data formatting | bytes 30720

commit v2 on v1

--- a/solution.py
+++ b/solution.py
@@ -27,7 +27,7 @@
 
 def kernel(
     n_row, n_col, classes, piece, group,
-    gram, targets, sol_out, res_out,
+    gram, targets, both_out,
     stage, high, low, acc, vec, wide,
     t_col, t_row, w_part, w_col, w_row, m_part, moments, finals,
     gram_sem, s_tcol, r_tcol, s_trow, r_trow, s_rs, r_rs, s_wcol, r_wcol, s_wrow, r_wrow,
@@ -52,12 +52,10 @@
 
     barrier = pltpu.get_barrier_semaphore()
 
-    def greet(k, carry):
-        other = lax.rem(row * n_col + col + k, n_dev)
-        pl.semaphore_signal(barrier, inc=1, device_id=(other // n_col, lax.rem(other, n_col)), device_id_type=MESH)
-        return carry
-
-    lax.fori_loop(1, n_dev, greet, 0)
+    for k in range(1, n_col):
+        pl.semaphore_signal(barrier, inc=1, device_id=(row, lax.rem(col + k, n_col)), device_id_type=MESH)
+    for k in range(1, n_row):
+        pl.semaphore_signal(barrier, inc=1, device_id=(lax.rem(row + k, n_row), col), device_id_type=MESH)
 
     rows8 = lax.broadcasted_iota(jnp.int32, (SUB, LANES), 0)
 
@@ -100,10 +98,20 @@
     mine_t = wide[...]
     t_col[0] = pack(mine_t)
     acc[...] = jnp.zeros_like(acc)
-    pl.semaphore_wait(barrier, n_dev - 1)
+    pl.semaphore_wait(barrier, n_row + n_col - 2)
 
     col_t = {k: go(to_col(t_col.at[0], t_col.at[k], s_tcol, r_tcol, k)) for k in range(1, n_col)}
     row_t = {k: go(to_row(t_col.at[0], t_row.at[k], s_trow, r_trow, k)) for k in range(1, n_row)}
+
+    def split(i):
+        pltpu.make_async_copy(gram.at[pl.ds(0, depth)], stage.at[i], gram_sem.at[i]).wait()
+
+        def part(j, carry):
+            off = pl.ds(pl.multiple_of(j * DEPTH, DEPTH), DEPTH)
+            high[i, off, :], low[i, off, :] = halves(stage[i, off, :])
+            return carry
+
+        lax.fori_loop(0, depth // DEPTH, part, 0)
 
     def gather(i, pieces, send, recv):
         for j in range(group):
@@ -122,19 +130,14 @@
         both = dot(v, h)
         acc[...] += both[:16] + both[16:] + dot(v[:16], l)
 
+    def product(i):
+        accumulate(vec[i], high[i], low[i])
+
     for i in range(n_group):
-        pltpu.make_async_copy(gram.at[pl.ds(0, depth)], stage.at[i], gram_sem.at[i]).wait()
+        split(i)
+    for i in range(n_group):
         gather(i, t_col, s_tcol, r_tcol)
-
-        def first(j, carry, i=i):
-            off = pl.ds(pl.multiple_of(j * DEPTH, DEPTH), DEPTH)
-            h, l = halves(stage[i, off, :])
-            high[i, off, :] = h
-            low[i, off, :] = l
-            accumulate(vec[i, :, off], h, l)
-            return carry
-
-        lax.fori_loop(0, depth // DEPTH, first, 0)
+        product(i)
 
     def columns(k):
         r = lax.rem(row - k + n_row, n_row)
@@ -159,68 +162,76 @@
     acc[...] = jnp.zeros_like(acc)
     mine_w = unpack(total)
 
+    def inner(xs, ys):
+        value = xs[0] * ys[0]
+        for x, y in zip(xs[1:], ys[1:]):
+            value = value + x * y
+        return jnp.sum(value, axis=1, keepdims=True)
+
+    lane = lax.broadcasted_iota(jnp.int32, (16, LANES), 1)
+    sub = lax.broadcasted_iota(jnp.int32, (16, LANES), 0)
+
+    def to_lanes(values):
+        out = jnp.zeros((16, LANES), F32)
+        for m, value in enumerate(values):
+            out = jnp.where(lane == sub + 16 * m, value, out)
+        return jnp.sum(out, axis=0, keepdims=True)
+
+    def from_lanes(line, m):
+        full = jnp.broadcast_to(line, (16, LANES))
+        return jnp.sum(jnp.where(lane == sub + 16 * m, full, 0.0), axis=1, keepdims=True)
+
+    tt, tw, ww = inner([mine_t], [mine_t]), inner([mine_t], [mine_w]), inner([mine_w], [mine_w])
+    guess = jnp.where(ww > 0.0, tw / jnp.where(ww > 0.0, ww, 1.0), 0.0)
+    near = mine_t - guess * mine_w
+    moments[0] = to_lanes([tt, tw, ww, guess, inner([near], [near]), inner([near], [mine_w])])
+
+    def to_all(lines, send, recv, k):
+        other = lax.rem(row * n_col + col + k, n_dev)
+        return pltpu.make_async_remote_copy(
+            src_ref=lines.at[0], dst_ref=lines.at[k], send_sem=send.at[k], recv_sem=recv.at[k],
+            device_id=(other // n_col, lax.rem(other, n_col)), device_id_type=MESH)
+
+    def loop_all(act, lines, send, recv):
+        def step(k, carry):
+            act(to_all(lines, send, recv, k))
+            return carry
+
+        lax.fori_loop(1, n_dev, step, 0)
+
+    loop_all(lambda c: c.start(), moments, s_mom, r_mom)
+
+    for i in range(n_group):
+        gather(i, w_col, s_wcol, r_wcol)
+        product(i)
+
+    rs2 = scatter(m_part, s_rs2, r_rs2)
+
     ts, ws = [mine_t], [mine_w]
     for k in range(1, n_row):
         row_t[k].wait_recv()
         row_w[k].wait_recv()
         ts.append(unpack(t_row[k]))
         ws.append(unpack(w_row[k]))
-
-    def inner(xs, ys):
-        value = xs[0] * ys[0]
-        for x, y in zip(xs[1:], ys[1:]):
-            value = value + x * y
-        return jnp.sum(value, axis=1, keepdims=True)
-
-    lane = lax.broadcasted_iota(jnp.int32, (16, LANES), 1)
-    sub = lax.broadcasted_iota(jnp.int32, (16, LANES), 0)
-
-    def to_lanes(values):
-        out = jnp.zeros((16, LANES), F32)
-        for m, value in enumerate(values):
-            out = jnp.where(lane == sub + 16 * m, value, out)
-        return jnp.sum(out, axis=0, keepdims=True)
-
-    def from_lanes(line, m):
-        full = jnp.broadcast_to(line, (16, LANES))
-        return jnp.sum(jnp.where(lane == sub + 16 * m, full, 0.0), axis=1, keepdims=True)
-
-    tt, tw, ww = inner(ts, ts), inner(ts, ws), inner(ws, ws)
-    guess = jnp.where(ww > 0.0, tw / jnp.where(ww > 0.0, ww, 1.0), 0.0)
-    rs0 = [t - guess * w for t, w in zip(ts, ws)]
-    rr, rw = inner(rs0, rs0), inner(rs0, ws)
-    moments[0] = to_lanes([tt, tw, ww, guess, rr, rw])
-    col_m = {k: go(to_col(moments.at[0], moments.at[k], s_mom, r_mom, k)) for k in range(1, n_col)}
-
-    for i in range(n_group):
-        gather(i, w_col, s_wcol, r_wcol)
-
-        def second(j, carry, i=i):
-            off = pl.ds(pl.multiple_of(j * DEPTH, DEPTH), DEPTH)
-            accumulate(vec[i, :, off], high[i, off, :], low[i, off, :])
-            return carry
-
-        lax.fori_loop(0, depth // DEPTH, second, 0)
-
-    rs2 = scatter(m_part, s_rs2, r_rs2)
-
-    for k in range(1, n_col):
-        col_m[k].wait_recv()
-    known = [[from_lanes(moments[k], m) for m in range(6)] for k in range(n_col)]
-
-    def add(values):
-        out = values[0]
-        for v in values[1:]:
-            out = out + v
-        return out
-
-    norm0 = add([m[0] for m in known])
-    t_k_t = add([m[1] for m in known])
-    step0 = norm0 / t_k_t
-    shift = [step0 - m[3] for m in known]
-    norm1 = add([m[4] - d * (2.0 * m[5] - d * m[2]) for m, d in zip(known, shift)])
-    r_w = add([m[5] - d * m[2] for m, d in zip(known, shift)])
-    beta = norm1 / norm0
+    loop_all(lambda c: c.wait_recv(), moments, s_mom, r_mom)
+    known = moments[...]
+
+    def moment(m):
+        return pltpu.roll(known, LANES - 16 * m, 2) if m else known
+
+    def total_of(value):
+        return jnp.sum(value, axis=0)
+
+    norm0_l = total_of(moment(0))
+    t_k_t_l = total_of(moment(1))
+    step0_l = norm0_l / t_k_t_l
+    shift = step0_l[None] - moment(3)
+    back = shift * moment(2)
+    norm1_l = total_of(moment(4) - shift * (2.0 * moment(5) - back))
+    r_w_l = total_of(moment(5) - back)
+    beta_l = norm1_l / norm0_l
+    fixed_l = (1.0 + beta_l) * (r_w_l + beta_l * t_k_t_l)
+    step0, norm1, beta, fixed = (from_lanes(x, 0) for x in (step0_l, norm1_l, beta_l, fixed_l))
 
     def direction(t, w):
         r = t - step0 * w
@@ -230,17 +241,7 @@
     ps = [acc[:, columns(k)] for k in range(n_row)]
     finals[0] = to_lanes([inner(ds, ps)])
 
-    def fin(k):
-        other = lax.rem(row * n_col + col + k, n_dev)
-        return pltpu.make_async_remote_copy(
-            src_ref=finals.at[0], dst_ref=finals.at[k], send_sem=s_fin.at[k], recv_sem=r_fin.at[k],
-            device_id=(other // n_col, lax.rem(other, n_col)), device_id_type=MESH)
-
-    def fin_start(k, carry):
-        fin(k).start()
-        return carry
-
-    lax.fori_loop(1, n_dev, fin_start, 0)
+    loop_all(lambda c: c.start(), finals, s_fin, r_fin)
 
     total2 = pack(acc[:, columns(0)])
     for k in range(1, n_row):
@@ -250,26 +251,23 @@
     r1, d1 = direction(mine_t, mine_w)
     mapped = (1.0 + beta) * mine_w - step0 * w2
 
-    def fin_wait(k, carry):
-        fin(k).wait_recv()
-        return carry
-
-    lax.fori_loop(1, n_dev, fin_wait, 0)
+    loop_all(lambda c: c.wait_recv(), finals, s_fin, r_fin)
     d_w2 = from_lanes(jnp.sum(finals[...], axis=0), 0)
-    step1 = norm1 / ((1.0 + beta) * (r_w + beta * t_k_t) - step0 * d_w2)
-    wide[...] = step0 * mine_t + step1 * d1
-    sol_out[...] = wide[0:classes, :]
-    wide[...] = r1 - step1 * mapped
-    res_out[...] = wide[0:classes, :]
+    step1 = norm1 / (fixed - step0 * d_w2)
+    both_out[0] = step0 * mine_t + step1 * d1
+    both_out[1] = r1 - step1 * mapped
 
     for copy in started:
         copy.wait_send()
 
-    def fin_sent(k, carry):
-        fin(k).wait_send()
-        return carry
-
-    lax.fori_loop(1, n_dev, fin_sent, 0)
+    loop_all(lambda c: c.wait_send(), moments, s_mom, r_mom)
+    loop_all(lambda c: c.wait_send(), finals, s_fin, r_fin)
+
+
+def apart(both, sol_out, res_out):
+    classes = sol_out.shape[0]
+    sol_out[...] = both[0, 0:classes, :]
+    res_out[...] = both[1, 0:classes, :]
 
 
 def fused(n_row, n_col, gram_matrix, targets):
@@ -282,11 +280,11 @@
     dma = pltpu.SemaphoreType.DMA
     n_dev = n_row * n_col
     vmem = pl.BlockSpec(memory_space=pltpu.VMEM)
-    return pl.pallas_call(
+    both = pl.pallas_call(
         functools.partial(kernel, n_row, n_col, classes, piece, group),
-        out_shape=[jax.ShapeDtypeStruct(targets.shape, F32)] * 2,
+        out_shape=jax.ShapeDtypeStruct((2, 16, piece), F32),
         in_specs=[pl.BlockSpec(memory_space=pl.ANY), vmem],
-        out_specs=[vmem, vmem],
+        out_specs=vmem,
         scratch_shapes=[
             pltpu.VMEM((n_group, depth, width), F32),
             pltpu.VMEM((n_group, depth, width), BF16),
@@ -300,20 +298,25 @@
             pltpu.VMEM((n_col,) + packed, F32),
             pltpu.VMEM((n_row,) + packed, F32),
             pltpu.VMEM((2 * n_row,) + packed, F32),
-            pltpu.VMEM((n_col, 1, LANES), F32),
+            pltpu.VMEM((n_dev, 1, LANES), F32),
             pltpu.VMEM((n_dev, 1, LANES), F32),
             dma((n_group,)),
             dma((n_col,)), dma((n_col,)), dma((n_row,)), dma((n_row,)),
             dma((n_row,)), dma((n_row,)),
             dma((n_col,)), dma((n_col,)), dma((n_row,)), dma((n_row,)),
             dma((n_row,)), dma((n_row,)),
-            dma((n_col,)), dma((n_col,)),
-            dma((n_dev,)), dma((n_dev,)),
+            dma((n_dev,)), dma((n_dev,)), dma((n_dev,)), dma((n_dev,)),
         ],
         compiler_params=pltpu.CompilerParams(
             collective_id=0, has_side_effects=True, vmem_limit_bytes=60 * 2**20
         ),
     )(gram_matrix, targets)
+    return pl.pallas_call(
+        apart,
+        out_shape=[jax.ShapeDtypeStruct(targets.shape, F32)] * 2,
+        in_specs=[vmem],
+        out_specs=[vmem, vmem],
+    )(both)
 
 
 def fits(n_row, n_col, gram_matrix, targets):

time: 37.4 us -> 33.8 us (0.904)
  local copies, waits for them, and re-layouts: 2.69 us -> 0 us
  Pallas kernels: 33.8 us -> 32.9 us
    unnamed x2 -> x0, local copies, waits for them, and re-layouts: 2.69 us -> none
    pallas_call x1, Pallas kernels: 33.8 us -> 31.5 us  [fused(): pl.pallas_call(functools.partial(kernel, n_row, n_col, classes, piece, gr...]
    pallas_call x0 -> x1, Pallas kernels: none -> 1.42 us  [fused(): pl.pallas_call(apart, out_shape=[jax.ShapeDtypeStruct(targets.shape, F32)...]
where the time goes in v2:
time: 33.8 us; the launch traced here: 33.5 us
  Pallas kernels  32.9 us (97%)
  between operations  0.64 us (2%)
    pallas_call x1, Pallas kernels, fused(): pl.pallas_call(functools.partial(kernel, n_row, n_col, classes, piece, gr...  31.5 us
    pallas_call x1, Pallas kernels, fused(): pl.pallas_call(apart, out_shape=[jax.ShapeDtypeStruct(targets.shape, F32)...  1.42 us

profile of v2, /device:TPU:0, one launch (start us, length us, event | category | flops | bytes accessed | tf_op | source)
XLA Modules:
  0.0 33.5 jit_solution(12916070399087294802)
XLA Ops:
  0.6 31.5 %shard_map.41.both = f32[2,16,384]{2,1,0:T(8,128)} custom-call(f32[3072,1536]{1,0:T(8,128)} %gram.1, f32[10,384]{1,0:T(8,128)} %targets.1), custom_call_target="tpu_custom_call" | custom-call | tf_op jit(solution)/shard_map/pallas_call | solution.py:283
  32.1 1.4 %shard_map.42 = (f32[10,384]{1,0:T(8,128)}, f32[10,384]{1,0:T(8,128)}) custom-call(f32[2,16,384]{2,1,0:T(8,128)} %shard_map.41.both), custom_call_target="tpu_custom_call" | custom-call | tf_op jit(solution)/shard_map/pallas_call | solution.py:314

commit v3 on v2

--- a/solution.py
+++ b/solution.py
@@ -87,6 +87,7 @@
             device_id=(lax.rem(row + k, n_row), col), device_id_type=MESH)
 
     started = []
+    far_first = sorted(range(1, n_col), key=lambda k: -min(k, n_col - k))
 
     def go(copy):
         copy.start()
@@ -100,7 +101,7 @@
     acc[...] = jnp.zeros_like(acc)
     pl.semaphore_wait(barrier, n_row + n_col - 2)
 
-    col_t = {k: go(to_col(t_col.at[0], t_col.at[k], s_tcol, r_tcol, k)) for k in range(1, n_col)}
+    col_t = {k: go(to_col(t_col.at[0], t_col.at[k], s_tcol, r_tcol, k)) for k in far_first}
     row_t = {k: go(to_row(t_col.at[0], t_row.at[k], s_trow, r_trow, k)) for k in range(1, n_row)}
 
     def split(i):
@@ -135,9 +136,17 @@
 
     for i in range(n_group):
         split(i)
-    for i in range(n_group):
+    for i in range(n_group - 1):
         gather(i, t_col, s_tcol, r_tcol)
         product(i)
+    gather(n_group - 1, t_col, s_tcol, r_tcol)
+
+    def product_of(k):
+        last = n_group - 1
+        r = lax.rem(row + k, n_row)
+        at = pl.ds(pl.multiple_of(r * piece, LANES), piece)
+        both = dot(vec[last], high[last, :, at])
+        return acc[:, at] + both[:16] + both[16:] + dot(vec[last, :16], low[last, :, at])
 
     def columns(k):
         r = lax.rem(row - k + n_row, n_row)
@@ -151,14 +160,17 @@
             copies[k] = go(to_row(parts.at[n_row + k], parts.at[k], send, recv, k))
         return copies
 
-    rs = scatter(w_part, s_rs, r_rs)
-    total = pack(acc[:, columns(0)])
+    rs = {}
+    for k in range(1, n_row):
+        w_part[n_row + k] = pack(product_of(k))
+        rs[k] = go(to_row(w_part.at[n_row + k], w_part.at[k], s_rs, r_rs, k))
+    total = pack(product_of(0))
     for k in range(1, n_row):
         rs[k].wait_recv()
         total = total + w_part[k]
     w_col[0] = total
-    col_w = {k: go(to_col(w_col.at[0], w_col.at[k], s_wcol, r_wcol, k)) for k in range(1, n_col)}
     row_w = {k: go(to_row(w_col.at[0], w_row.at[k], s_wrow, r_wrow, k)) for k in range(1, n_row)}
+    col_w = {k: go(to_col(w_col.at[0], w_col.at[k], s_wcol, r_wcol, k)) for k in far_first}
     acc[...] = jnp.zeros_like(acc)
     mine_w = unpack(total)
 
@@ -197,15 +209,14 @@
             act(to_all(lines, send, recv, k))
             return carry
 
-        lax.fori_loop(1, n_dev, step, 0)
+        for k in range(1, n_dev):
+            step(k, 0)
 
     loop_all(lambda c: c.start(), moments, s_mom, r_mom)
 
-    for i in range(n_group):
+    for i in range(n_group - 1):
         gather(i, w_col, s_wcol, r_wcol)
         product(i)
-
-    rs2 = scatter(m_part, s_rs2, r_rs2)
 
     ts, ws = [mine_t], [mine_w]
     for k in range(1, n_row):
@@ -238,11 +249,14 @@
         return r, r + beta * t
 
     ds = [direction(t, w)[1] for t, w in zip(ts, ws)]
+    gather(n_group - 1, w_col, s_wcol, r_wcol)
+    product(n_group - 1)
     ps = [acc[:, columns(k)] for k in range(n_row)]
     finals[0] = to_lanes([inner(ds, ps)])
 
     loop_all(lambda c: c.start(), finals, s_fin, r_fin)
 
+    rs2 = scatter(m_part, s_rs2, r_rs2)
     total2 = pack(acc[:, columns(0)])
     for k in range(1, n_row):
         rs2[k].wait_recv()

time: 33.8 us -> 33.2 us (0.982)
  Pallas kernels: 32.9 us -> 32.3 us
    pallas_call x1, Pallas kernels: 31.5 us -> 30.9 us  [fused(): pl.pallas_call(functools.partial(kernel, n_row, n_col, classes, piece, gr...]
where the time goes in v3:
time: 33.2 us; the launch traced here: 32.9 us
  Pallas kernels  32.3 us (97%)
  between operations  0.64 us (2%)
    pallas_call x1, Pallas kernels, fused(): pl.pallas_call(functools.partial(kernel, n_row, n_col, classes, piece, gr...  30.9 us
    pallas_call x1, Pallas kernels, fused(): pl.pallas_call(apart, out_shape=[jax.ShapeDtypeStruct(targets.shape, F32)...  1.42 us

profile of v3, /device:TPU:0, one launch (start us, length us, event | category | flops | bytes accessed | tf_op | source)
XLA Modules:
  0.0 32.9 jit_solution(12879546018687653599)
XLA Ops:
  0.6 30.9 %shard_map.41.both = f32[2,16,384]{2,1,0:T(8,128)} custom-call(f32[3072,1536]{1,0:T(8,128)} %gram.1, f32[10,384]{1,0:T(8,128)} %targets.1), custom_call_target="tpu_custom_call" | custom-call | tf_op jit(solution)/shard_map/pallas_call | solution.py:297
  31.5 1.4 %shard_map.42 = (f32[10,384]{1,0:T(8,128)}, f32[10,384]{1,0:T(8,128)}) custom-call(f32[2,16,384]{2,1,0:T(8,128)} %shard_map.41.both), custom_call_target="tpu_custom_call" | custom-call | tf_op jit(solution)/shard_map/pallas_call | solution.py:328
